TPU v7x, 128 devices: a whole 4x4x4 slice. The times are simulated.
128 devices in a mesh: tm: 8 (over x_hi, z), chan: 16 (over y, x_lo, core).
Axes of the slice: x: 4 (x_hi: 2, x_lo: 2; x = x_hi * 2 + x_lo), y: 4, z: 4, core: 2. Of those that a mesh axis runs over, the one named last changes fastest.
Arguments:
- raw_data: float32 [10240, 6144], P('tm', 'chan'), may hold values from -6 to 6
- fir_taps: float32 [33], replicated, may hold values from -1 to 1
- spectral_weight: float32 [64], replicated, may hold values from 0.1 to 1
Outputs:
- correlations: float32 [128, 201, 10240], P('chan', None, 'tm')
All inputs are finite; a program needn't handle non-finite values.
Results may differ from a plain program's by a relative error of at most 0.0034.
Values may be sent and summed in bfloat16 or wider, within the bound.
A program may use at most 192 MiB of HBM per device.

v0:
```python
import functools

import jax
import jax.numpy as jnp
import ml_dtypes
import numpy as np
from jax import lax
from jax.experimental import pallas as pl
from jax.experimental.pallas import tpu as pltpu
from jax.sharding import PartitionSpec as P

HK = 16
TN = 64
SEG = 128
HALF = 100
LAGS = 201
LPAD = 208
EPS = 1e-06
FLOOR = 0.5
HALO = HK + TN
BF = jnp.bfloat16
F32 = jnp.float32


def split_np(table):
    table = np.asarray(table, np.float32)
    hi = table.astype(ml_dtypes.bfloat16)
    lo = (table - hi.astype(np.float32)).astype(ml_dtypes.bfloat16)
    return hi, lo


def tables():
    t, f = np.arange(SEG), np.arange(SEG // 2)
    angle = 2.0 * np.pi * ((t[:, None] * f[None, :]) % SEG) / SEG
    forward = np.concatenate([np.cos(angle), np.sin(angle)], axis=1)
    weight = np.where(f == 0, 1.0, 2.0)[:, None]
    inverse = np.concatenate([np.cos(angle).T * weight, np.sin(angle).T * weight]) / np.sqrt(SEG)
    stacked = []
    for table in (forward, inverse):
        row = np.concatenate(split_np(table), axis=1)
        stacked.append(np.concatenate([row, row], axis=0))
    i, o = np.arange(384)[:, None], np.arange(256)[None, :]
    band = ((i - o >= 0) & (i - o <= 2 * TN)).astype(ml_dtypes.bfloat16)
    mean = np.full((256, 128), 1.0 / 128, ml_dtypes.bfloat16)
    return stacked[0], stacked[1], band, mean


def dot(a, b):
    return jnp.dot(a, b, preferred_element_type=F32)


def split2(x):
    hi = x.astype(BF)
    return hi, (x - hi.astype(F32)).astype(BF)


def split3(x):
    hi = x.astype(BF)
    rest = x - hi.astype(F32)
    mid = rest.astype(BF)
    return hi, mid, (rest - mid.astype(F32)).astype(BF)


def front_kernel(raw, left, right, toep, weight, fwd, inv, band, mean, out, ext, t_hi, t_mid, t_lo):
    chan = lax.axis_index("chan")
    ends = lax.axis_size("chan") - 1

    @pl.when(pl.program_id(0) == 0)
    def _():
        hi, mid, lo = split3(toep[...])
        t_hi[...] = hi
        t_mid[...] = mid
        t_lo[...] = lo

    n = raw.shape[1]
    ext[:, 0:HALO] = left[...]
    ext[:, HALO : HALO + n] = raw[...]
    ext[:, HALO + n : 2 * HALO + n] = right[...]
    ext[:, 2 * HALO + n :] = jnp.zeros((ext.shape[0], ext.shape[1] - 2 * HALO - n), F32)

    def fir(x):
        hi, mid, lo = split3(x)
        small = dot(mid, t_mid[...]) + dot(hi, t_lo[...]) + dot(lo, t_hi[...])
        return (small + (dot(hi, t_mid[...]) + dot(mid, t_hi[...]))) + dot(hi, t_hi[...])

    f = jnp.concatenate([fir(ext[:, 0:384]), fir(ext[:, 256:640])], axis=1)
    lane = lax.broadcasted_iota(jnp.int32, (1, 512), 1)
    low = jnp.where(chan == 0, TN, 0)
    high = jnp.where(chan == ends, TN + n, 512)
    f = jnp.where((lane >= low) & (lane < high), f, 0.0)
    hi, lo = split2(jnp.abs(f))
    first = dot(hi[:, 0:384], band[...]) + dot(lo[:, 0:384], band[...])
    second = dot(hi[:, 256:512], band[0:256, 0:128]) + dot(lo[:, 256:512], band[0:256, 0:128])
    summed = jnp.concatenate([first, second], axis=1)
    norm = f[:, TN : TN + n] / (summed * (1.0 / (2 * TN + 1)) + EPS)
    for s in range(n // SEG):
        x = norm[:, s * SEG : (s + 1) * SEG]
        p = dot(jnp.concatenate(split2(x), axis=1), fwd[...])
        spec = p[:, :SEG] + p[:, SEG:]
        sq = spec * spec
        amp = jnp.sqrt(sq + pltpu.roll(sq, SEG // 2, 1))
        mean_amp = dot(jnp.concatenate(split2(amp), axis=1), mean[...]) + EPS
        z = spec * (weight[...] / jnp.maximum(amp, FLOOR * mean_amp))
        q = dot(jnp.concatenate(split2(z), axis=1), inv[...])
        out[:, s * SEG : (s + 1) * SEG] = (q[:, :SEG] + q[:, SEG:]).astype(BF)


def front(raw, left, right, toep, weight, rows=256):
    count, n = raw.shape
    fwd, inv, band, mean = (jnp.asarray(t) for t in tables())
    whole = lambda a: pl.BlockSpec(a.shape, lambda i: (0,) * a.ndim)
    blk = lambda w: pl.BlockSpec((rows, w), lambda i: (i, 0))
    return pl.pallas_call(
        front_kernel,
        grid=(count // rows,),
        in_specs=[blk(n), blk(HALO), blk(HALO)] + [whole(a) for a in (toep, weight, fwd, inv, band, mean)],
        out_specs=blk(n),
        out_shape=jax.ShapeDtypeStruct((count, n), BF),
        scratch_shapes=[pltpu.VMEM((rows, 640), F32)] + [pltpu.VMEM((384, 256), BF)] * 3,
        compiler_params=pltpu.CompilerParams(vmem_limit_bytes=40 << 20),
        name="front",
    )(raw, left, right, toep, weight, fwd, inv, band, mean)


def corr_kernel(src, rec, out, lagged):
    count, total = src.shape[0], rec.shape[1]
    blocks = total // 128

    @pl.when(pl.program_id(0) == 0)
    def _():
        @pl.loop(0, count)
        def _(k):
            base = pl.multiple_of(k * LPAD, 16)
            for j in range(-1, blocks):
                row = src[pl.ds(k, 1), pl.ds((j + 1) * 128, 256)]
                rolled = pltpu.roll(jnp.broadcast_to(row, (128, 256)), 0, 1, stride=1, stride_axis=0)
                tile = rolled[:, 128:].astype(BF)
                if j >= 0:
                    lagged[pl.ds(base, 128), j * 128 : (j + 1) * 128] = tile
                if j < blocks - 1:
                    lagged[pl.ds(base + 128, LPAD - 128), (j + 1) * 128 : (j + 2) * 128] = tile[: LPAD - 128]

    scale = total**-0.5

    @pl.loop(0, count)
    def _(k):
        base = pl.multiple_of(k * LPAD, 16)
        acc = lax.dot_general(
            lagged[pl.ds(base, LPAD), :], rec[...], (((1,), (1,)), ((), ())), preferred_element_type=F32
        )
        out[k] = acc[:LAGS] * scale


def corr(src, rec, cols=256):
    total_rec, total = rec.shape
    count = src.shape[0]
    return pl.pallas_call(
        corr_kernel,
        grid=(total_rec // cols,),
        in_specs=[
            pl.BlockSpec(src.shape, lambda i: (0, 0)),
            pl.BlockSpec((cols, total), lambda i: (i, 0)),
        ],
        out_specs=pl.BlockSpec((count, LAGS, cols), lambda i: (0, 0, i)),
        out_shape=jax.ShapeDtypeStruct((count, LAGS, total_rec), F32),
        scratch_shapes=[pltpu.VMEM((count * LPAD, total), BF)],
        compiler_params=pltpu.CompilerParams(vmem_limit_bytes=56 << 20),
        name="corr",
    )(src, rec)


def lag_source(sources):
    total = sources.shape[1]
    left = 256 - HALF
    return jnp.pad(sources, ((0, 0), (left, HALF))).astype(F32)


def toeplitz(fir_taps):
    diff = lax.broadcasted_iota(jnp.int32, (384, 256), 0) - lax.broadcasted_iota(jnp.int32, (384, 256), 1)
    out = jnp.zeros((384, 256), F32)
    for k in range(fir_taps.shape[0]):
        out = jnp.where(diff == k, fir_taps[k], out)
    return out


def shards(raw_data, fir_taps, spectral_weight):
    channels_dev, samples_dev = raw_data.shape
    chan_count = lax.axis_size("chan")
    tm_count = lax.axis_size("tm")
    ends = chan_count - 1
    left = lax.ppermute(raw_data[:, samples_dev - HALO :], "chan", [(i, i + 1) for i in range(ends)])
    right = lax.ppermute(raw_data[:, :HALO], "chan", [(i + 1, i) for i in range(ends)])
    weight = jnp.concatenate([spectral_weight, spectral_weight])[None, :]
    whitened = front(raw_data, left, right, toeplitz(fir_taps), weight)
    source_dev = 128 // chan_count
    stride = channels_dev * tm_count // 128
    own = whitened[::stride]
    every = lax.all_gather(own, "chan", axis=1, tiled=True)
    every = lax.all_gather(every, "tm", axis=0, tiled=True)
    sources = lax.dynamic_slice_in_dim(every, lax.axis_index("chan") * source_dev, source_dev, 0)
    receivers = lax.all_gather(whitened, "chan", axis=1, tiled=True)
    return corr(lag_source(sources), receivers)


def solution(mesh):
    in_specs = (P("tm", "chan"), P(), P())
    out_specs = P("chan", None, "tm")
    return jax.shard_map(shards, mesh=mesh, in_specs=in_specs, out_specs=out_specs, check_vma=False)
```

profile of v0, /device:TPU:1, one launch (start us, length us, event | category | flops | bytes accessed | tf_op | source)
XLA Modules:
  0.0 294.5 jit_solution(17148358401283002595)
XLA Ops:
  6.5 1.6 fusion.33
  8.1 0.2 copy.14
  8.3 0.0 copy-start
  8.3 0.0 copy-start.2
  8.3 4.6 %collective-permute-start = (f32[1280,80]{0,1:T(8,128)S(1)}, f32[1280,80]{0,1:T(8,128)}, u32[]{:S(2)}, u32[]{:S(2)}) collective-permute-start(f32[1280,80]{0,1:T(8,128)S(1)} %copy.14), channel_id=1, source_target_pairs={{0,1},{1,2},{2,3},{3,4},{4,5},{5,6},{6,7},{7,8},{8,9},{9,10},{10,1... | collective-permute-start | bytes 1228808 | tf_op jit(solution)/shard_map/ppermute | solution.py:191
  13.0 1.0 copy.15
  14.0 1.9 collective-permute-start.1
  15.9 0.7 fusion.35
  16.6 0.0 copy-done.6
  16.6 0.1 maximum_bitcast_fusion.weight
  16.7 0.7 fusion.34
  17.4 21.7 %select_select_fusion.toep = f32[384,256]{1,0:T(8,128)} fusion(f32[]{:T(128)} %bitcast.32, f32[]{:T(128)} %bitcast.31, f32[]{:T(128)} %bitcast.30, f32[]{:T(128)} %bitcast.29, f32[]{:T(128)} %bitcast.28, f32[]{:T(128)} %bitcast.27, f32[]{:T(128)} %bitcast.26, f32[]{:T(128)} %bitcast.25, f32[]{:T(128)} %bitcast.24, f32[]{:T(128)} %bitcast.23, f32[]{:T(128)} %bitcast.22, ...), kind=kLoop, calls=%fused_computation | loop fusion | flops 6586368 | bytes 393348 | tf_op jit(solution)/shard_map/jit(_where)/select_n | solution.py:182
  39.1 0.0 collective-permute-done
  39.1 1.2 copy.11.left
  40.3 0.0 collective-permute-done.1
  40.3 1.2 copy.12.right
  41.6 0.0 copy-done
  41.6 1.0 copy-done.1
  42.6 0.9 copy-done.3
  43.5 0.9 copy-done.4
  44.4 14.0 %front.1 = bf16[1280,384]{1,0:T(8,128)(2,1)} custom-call(f32[1280,384]{1,0:T(8,128)S(1)} %copy-done, f32[1280,80]{1,0:T(8,128)S(1)} %copy.11.left, f32[1280,80]{1,0:T(8,128)S(1)} %copy.12.right, f32[384,256]{1,0:T(8,128)S(1)} %copy-done.1, f32[1,128]{1,0:T(1,128)S(1)} %maximum_bitcast_fusion.weight, bf16[256,256]{1,0:T(8,128)(2,1)S(1)} %copy-done.4, ...), custom_call_target="tpu_custom_call" | custom-call | tf_op jit(solution)/shard_map/front/pallas_call | solution.py:113
  58.4 1.2 slice.143
  59.6 22.5 %all_gather.9 = bf16[16,6144]{1,0:T(8,128)(2,1)} all-gather(bf16[16,384]{1,0:T(8,128)(2,1)S(1)} %slice.143), channel_id=1, replica_groups=mesh['tm'=8,'chan'=16] {'chan'}, dimensions={1}, use_global_device_ids=true | all-gather | bytes 208896 | tf_op jit(solution)/shard_map/all_gather | solution.py:198
  82.1 0.0 all-gather.3.cloned.1.call-update
  82.2 0.0 all-gather.5.cloned.1.call-start
  82.2 0.7 all-gather.5.cloned.1.call-update
  82.9 47.6 %all-gather.3.cloned.1.call-done = bf16[128,6144]{1,0:T(8,128)(2,1)} async-done(((bf16[16,6144]{1,0:T(8,128)(2,1)}), bf16[128,6144]{1,0:T(8,128)(2,1)}) %all-gather.3.cloned.1.call-update) | async-done | bytes 1572880 | tf_op jit(solution)/shard_map/all_gather | solution.py:199
  130.6 0.9 constant_dynamic-slice_fusion
  131.5 0.8 pad_convert_fusion.src
  132.2 86.1 %all-gather.5.cloned.1.call-done.rec = bf16[1280,6144]{1,0:T(8,128)(2,1)} async-done(((bf16[1280,384]{1,0:T(8,128)(2,1)}), bf16[1280,6144]{1,0:T(8,128)(2,1)}) %all-gather.5.cloned.1.call-update) | async-done | bytes 15728656 | tf_op jit(solution)/shard_map/all_gather | solution.py:201
  218.3 57.8 %corr.1 = f32[8,201,1280]{2,1,0:T(8,128)} custom-call(f32[8,6400]{1,0:T(8,128)} %pad_convert_fusion.src, bf16[1280,6144]{1,0:T(8,128)(2,1)} %all-gather.5.cloned.1.call-done.rec), custom_call_target="tpu_custom_call" | custom-call | tf_op jit(solution)/shard_map/corr/pallas_call | solution.py:157
  276.1 11.5 %copy.13 = f32[8,201,1280]{2,0,1:T(8,128)} copy(f32[8,201,1280]{2,1,0:T(8,128)} %corr.1) | data formatting | bytes 16465920 | tf_op jit(solution)/shard_map/corr/pallas_call | solution.py:157
  (9 shorter events, 0.0 us)
Async XLA Ops:
  6.5 9.4 %copy-start.5 = (f32[33]{0:T(128)S(1)}, f32[33]{0:T(128)}, u32[]{:S(2)}) copy-start(f32[33]{0:T(128)} %param.8) | copy-start | bytes 400
  6.5 10.1 %copy-start.6 = (f32[64]{0:T(128)S(1)}, f32[64]{0:T(128)}, u32[]{:S(2)}) copy-start(f32[64]{0:T(128)} %param.9) | copy-start | bytes 772
  6.5 124.0 %all-gather.3.cloned.1.call-start = ((), (), s32[]{:S(2)}) async-start(), calls=%async_computation | async-start | bytes 1769472 | tf_op jit(solution)/shard_map/all_gather | solution.py:199
  8.3 33.3 %copy-start = (f32[1280,384]{1,0:T(8,128)S(1)}, f32[1280,384]{1,0:T(8,128)}, u32[]{:S(2)}) copy-start(f32[1280,384]{1,0:T(8,128)} %raw.1) | copy-start | bytes 5898244
  8.3 33.3 %copy-start.2 = (bf16[384,256]{1,0:T(8,128)(2,1)S(1)}, bf16[384,256]{1,0:T(8,128)(2,1)}, u32[]{:S(2)}) copy-start(bf16[384,256]{1,0:T(8,128)(2,1)} %constant.88.clone.band) | copy-start | bytes 589828
  8.3 30.7 %collective-permute-start = (f32[1280,80]{0,1:T(8,128)S(1)}, f32[1280,80]{0,1:T(8,128)}, u32[]{:S(2)}, u32[]{:S(2)}) collective-permute-start(f32[1280,80]{0,1:T(8,128)S(1)} %copy.14), channel_id=1, source_target_pairs={{0,1},{1,2},{2,3},{3,4},{4,5},{5,6},{6,7},{7,8},{8,9},{9,10},{10,1... | collective-permute-start | bytes 1228808 | tf_op jit(solution)/shard_map/ppermute | solution.py:191
  14.0 26.4 %collective-permute-start.1 = (f32[1280,80]{0,1:T(8,128)}, f32[1280,80]{0,1:T(8,128)}, u32[]{:S(2)}, u32[]{:S(2)}) collective-permute-start(f32[1280,80]{0,1:T(8,128)} %copy.15), channel_id=1, source_target_pairs={{1,0},{2,1},{3,2},{4,3},{5,4},{6,5},{7,6},{8,7},{9,8},{10,9},{11,1... | collective-permute-start | bytes 1228808 | tf_op jit(solution)/shard_map/ppermute | solution.py:192
  41.6 1.0 copy-start.1
  42.6 0.9 copy-start.3
  43.5 0.9 copy-start.4
  82.2 136.2 %all-gather.5.cloned.1.call-start = ((), (), s32[]{:S(2)}) async-start(), calls=%async_computation.1 | async-start | bytes 16711680 | tf_op jit(solution)/shard_map/all_gather | solution.py:201
Sparse Core Ops, SparseCore 0:
  82.3 48.2 all-gather.2
  132.2 86.0 all-gather.4
where the time goes:
time: 295 us; the launch traced here: 294 us
  waiting for transfers between devices  134 us (45%)
  Pallas kernels  71.8 us (24%)
  local copies, waits for them, and re-layouts  23.1 us (8%)
  other arithmetic  22.5 us (8%)
  blocking collectives  22.5 us (8%)
  between operations  13.5 us (5%)
  starting transfers between devices  6.6 us (2%)
    all_gather x1, waiting for transfers between devices, shards(): receivers = lax.all_gather(whitened, 'chan', axis=1, tiled=True)  86.1 us
    pallas_call x1, Pallas kernels, corr(): pl.pallas_call(corr_kernel, grid=(total_rec // cols,), in_specs=[pl.Block...  57.8 us
    all_gather x1, waiting for transfers between devices, shards(): every = lax.all_gather(every, 'tm', axis=0, tiled=True)  47.6 us
    all_gather x1, blocking collectives, shards(): every = lax.all_gather(own, 'chan', axis=1, tiled=True)  22.5 us
    select_n x1, other arithmetic, toeplitz(): out = jnp.where(diff == k, fir_taps[k], out)  21.7 us
    pallas_call x1, Pallas kernels, front(): pl.pallas_call(front_kernel, grid=(count // rows,), in_specs=[blk(n), blk...  14 us
    pallas_call x1, local copies, waits for them, and re-layouts, corr(): pl.pallas_call(corr_kernel, grid=(total_rec // cols,), in_specs=[pl.Block...  11.5 us
  transfers between devices with their start and end apart: 4, of which 2 were waited for; matrix products, arithmetic and copies ran while one was open for 9% of the time, Pallas kernels for 0%

commit v1 on v0

--- a/solution.py
+++ b/solution.py
@@ -1,5 +1,3 @@
-import functools
-
 import jax
 import jax.numpy as jnp
 import ml_dtypes
@@ -14,7 +12,6 @@
 SEG = 128
 HALF = 100
 LAGS = 201
-LPAD = 208
 EPS = 1e-06
 FLOOR = 0.5
 HALO = HK + TN
@@ -67,7 +64,8 @@
 
     @pl.when(pl.program_id(0) == 0)
     def _():
-        hi, mid, lo = split3(toep[...])
+        rows = jnp.broadcast_to(toep[...], (256, 384))
+        hi, mid, lo = split3(pltpu.roll(rows, 0, 1, stride=1, stride_axis=0).T)
         t_hi[...] = hi
         t_mid[...] = mid
         t_lo[...] = lo
@@ -122,65 +120,290 @@
     )(raw, left, right, toep, weight, fwd, inv, band, mean)
 
 
-def corr_kernel(src, rec, out, lagged):
-    count, total = src.shape[0], rec.shape[1]
+WIDE = 384
+COLS = 256
+PIECES = 4
+
+
+def build_lags(z, lagged, total):
+    lane = lax.broadcasted_iota(jnp.int32, (8, 128), 1)
     blocks = total // 128
 
-    @pl.when(pl.program_id(0) == 0)
+    @pl.loop(0, 64)
+    def _(p):
+        shift = p * 2
+        tiles = []
+        for one in (shift, shift + 1):
+            rolled = [pltpu.roll(z[:, j * 128 : (j + 1) * 128], one, 1) for j in range(1, blocks + 3)]
+            tiles.append([jnp.where(lane < one, rolled[j], rolled[j + 1]) for j in range(blocks + 1)])
+        pairs = [jnp.concatenate([tiles[0][j], tiles[1][j]], axis=0).astype(BF) for j in range(blocks + 1)]
+
+        @pl.when(shift + HALF < LAGS)
+        def _():
+            row = pl.ds(pl.multiple_of((shift + HALF) * 8, 16), 16)
+            for j in range(blocks):
+                lagged[row, j * 128 : (j + 1) * 128] = pairs[j]
+
+        @pl.when(shift >= 128 - HALF)
+        def _():
+            row = pl.ds(pl.multiple_of((shift - (128 - HALF)) * 8, 16), 16)
+            for j in range(blocks):
+                lagged[row, j * 128 : (j + 1) * 128] = pairs[j + 1]
+
+
+def corr_kernel(wh, own_src, out, rec, lagged, z, stage, own_sem, send, recv, src_send, src_recv, out_sem):
+    tm, me = lax.axis_index("tm"), lax.axis_index("chan")
+    n_tm, n_chan = lax.axis_size("tm"), lax.axis_size("chan")
+    count, n = wh.shape
+    total = n * n_chan
+    chunks = count // COLS
+    y, x, core = me // 4, (me // 2) % 2, me % 2
+    n_y = n_chan // 4
+    up, down, far = (y + 1) % n_y, (y + n_y - 1) % n_y, (y + 2) % n_y
+
+    def at(yy, xx, cc):
+        return (yy * 2 + xx) * 2 + cc
+
+    to_x, to_u, to_d, to_s = at(y, 1 - x, core), at(up, x, core), at(down, x, core), at(y, x, 1 - core)
+
+    def lanes(b):
+        return pl.ds(pl.multiple_of(b * n, 128), n)
+
+    def signal(t, c):
+        pl.semaphore_signal(
+            pltpu.get_barrier_semaphore(), inc=1, device_id=(t, c), device_id_type=pl.DeviceIdType.MESH
+        )
+
+    per = n_chan // n_tm
+    targets = [(t, per * tm + h) for t in range(n_tm) for h in range(per)]
+    origins = [(me // per, c) for c in range(n_chan)]
+    for t, c in targets + origins:
+
+        @pl.when((t != tm) | (c != me))
+        def _():
+            signal(t, c)
+
+    for c in (to_x, to_u, to_d, to_s):
+        signal(tm, c)
+    barrier = pltpu.get_barrier_semaphore()
+    mine = me // per == tm
+
+    @pl.when(mine)
     def _():
-        @pl.loop(0, count)
-        def _(k):
-            base = pl.multiple_of(k * LPAD, 16)
-            for j in range(-1, blocks):
-                row = src[pl.ds(k, 1), pl.ds((j + 1) * 128, 256)]
-                rolled = pltpu.roll(jnp.broadcast_to(row, (128, 256)), 0, 1, stride=1, stride_axis=0)
-                tile = rolled[:, 128:].astype(BF)
-                if j >= 0:
-                    lagged[pl.ds(base, 128), j * 128 : (j + 1) * 128] = tile
-                if j < blocks - 1:
-                    lagged[pl.ds(base + 128, LPAD - 128), (j + 1) * 128 : (j + 2) * 128] = tile[: LPAD - 128]
-
+        pl.semaphore_wait(barrier, len(targets) + len(origins) + 2)
+
+    @pl.when(jnp.logical_not(mine))
+    def _():
+        pl.semaphore_wait(barrier, len(targets) + len(origins) + 4)
+
+    def src_copy(t, c, h, send_slot, who):
+        return pltpu.make_async_remote_copy(
+            src_ref=own_src.at[h * 8 : (h + 1) * 8, :],
+            dst_ref=z.at[:, pl.ds(pl.multiple_of(256 + who * n, 128), n)],
+            send_sem=src_send.at[send_slot],
+            recv_sem=src_recv.at[who],
+            device_id=(t, c),
+            device_id_type=pl.DeviceIdType.MESH,
+        )
+
+    for slot, (t, c) in enumerate(targets):
+
+        @pl.when((t != tm) | (c != me))
+        def _():
+            src_copy(t, c, slot % per, slot, me).start()
+
+    def copy(s_kind, r_kind, c, target, block, half=None, source=None):
+        size = COLS if half is None else COLS // 2
+        start = c * COLS + (0 if half is None else half * size)
+        rows = pl.ds(pl.multiple_of(start, 128), size)
+        return pltpu.make_async_remote_copy(
+            src_ref=rec.at[rows, lanes(block)] if source is None else source.at[rows, :],
+            dst_ref=rec.at[rows, lanes(block)],
+            send_sem=send.at[s_kind, c],
+            recv_sem=recv.at[r_kind, c],
+            device_id=(tm, target),
+            device_id_type=pl.DeviceIdType.MESH,
+        )
+
+    blk_p, blk_u, blk_d = at(y, 1 - x, core), at(up, x, core), at(down, x, core)
+    blk_up, blk_dp = at(up, 1 - x, core), at(down, 1 - x, core)
+    blk_f, blk_fp = at(far, x, core), at(far, 1 - x, core)
+
+    def sends(c, name):
+        table = {
+            "own": [
+                (0, 0, c, to_x, me, None, wh),
+                (1, 2, c, to_u, me, None, wh),
+                (2, 1, c, to_d, me, None, wh),
+                (3, 8, c, to_s, me, None, wh),
+            ],
+            "p": [(4, 4, c, to_u, blk_p), (5, 3, c, to_d, blk_p), (6, 9, c, to_s, blk_p)],
+            "u": [(7, 6, c, to_d, blk_u, 1), (8, 10, c, to_s, blk_u)],
+            "d": [(9, 5, c, to_u, blk_d, 0), (10, 11, c, to_s, blk_d)],
+            "f": [(11, 7, c, to_x, blk_f), (12, 14, c, to_s, blk_f)],
+            "up": [(13, 12, c, to_s, blk_up)],
+            "dp": [(14, 13, c, to_s, blk_dp)],
+            "fp": [(15, 15, c, to_s, blk_fp)],
+        }
+        return [copy(*one) for one in table[name]]
+
+    def start(c, *names):
+        for name in names:
+            for one in sends(c, name):
+                one.start()
+
+    def arrived(c, r_kind, block, half=None):
+        copy(0, r_kind, c, to_x, block, half=half).wait_recv()
+
+    own_copy = pltpu.make_async_copy(wh, rec.at[:, lanes(me)], own_sem)
+    start(0, "own")
+    own_copy.start()
+    z[:, 0:256] = jnp.zeros((8, 256), F32)
+    z[:, 256 + total :] = jnp.zeros((8, 128), F32)
+
+    @pl.when(mine)
+    def _():
+        z[:, pl.ds(pl.multiple_of(256 + me * n, 128), n)] = own_src[pl.ds(pl.multiple_of((me % per) * 8, 8), 8), :]
+
+    start(1, "own")
+    own_copy.wait()
+    for c in range(n_chan):
+
+        @pl.when((me // per != tm) | (c != me))
+        def _():
+            src_copy(tm, to_x, 0, 0, c).wait_recv()
+
+    build_lags(z, lagged, total)
     scale = total**-0.5
-
-    @pl.loop(0, count)
-    def _(k):
-        base = pl.multiple_of(k * LPAD, 16)
+    used = LAGS * 8
+    step = -(-used // PIECES // 16) * 16
+
+    def out_copy(c):
+        return pltpu.make_async_copy(
+            stage.at[c % 2], out.at[:, :, pl.ds(pl.multiple_of(c * COLS, 128), COLS)], out_sem.at[c % 2]
+        )
+
+    def piece(c, i):
+        first = i * step
+        rows = min(step, used - first)
+        full = -(-rows // 16) * 16
         acc = lax.dot_general(
-            lagged[pl.ds(base, LPAD), :], rec[...], (((1,), (1,)), ((), ())), preferred_element_type=F32
+            lagged[first : first + full, :],
+            rec[pl.ds(pl.multiple_of(c * COLS, 128), COLS), :],
+            (((1,), (1,)), ((), ())),
+            preferred_element_type=F32,
         )
-        out[k] = acc[:LAGS] * scale
-
-
-def corr(src, rec, cols=256):
-    total_rec, total = rec.shape
-    count = src.shape[0]
+        stage[c % 2, first // 8 : (first + rows) // 8] = (acc[:rows] * scale).reshape(rows // 8, 8, COLS)
+
+    @pl.loop(0, chunks + 1)
+    def _(c):
+        live, ready = c < chunks, c >= 1
+        b = c - 1
+
+        @pl.when(live & (c >= 1) & (c + 1 < chunks))
+        def _():
+            start(c + 1, "own")
+
+        @pl.when(live)
+        def _():
+            arrived(c, 0, blk_p)
+            start(c, "p")
+
+        @pl.when(ready)
+        def _():
+            for kind, yy in ((8, y), (9, y), (10, up), (11, down), (12, up), (13, down), (14, far), (15, far)):
+                xx = x if kind in (8, 10, 11, 14) else 1 - x
+                arrived(b, kind, at(yy, xx, 1 - core))
+
+            @pl.when(b >= 2)
+            def _():
+                out_copy(b - 2).wait()
+
+            piece(b, 0)
+
+        @pl.when(live)
+        def _():
+            arrived(c, 1, blk_u)
+            start(c, "u")
+            arrived(c, 2, blk_d)
+            start(c, "d")
+
+        @pl.when(ready)
+        def _():
+            piece(b, 1)
+
+        @pl.when(live)
+        def _():
+            arrived(c, 5, blk_f, half=0)
+            arrived(c, 6, blk_f, half=1)
+            start(c, "f")
+
+        @pl.when(ready)
+        def _():
+            piece(b, 2)
+
+        @pl.when(live)
+        def _():
+            arrived(c, 3, blk_up)
+            start(c, "up")
+            arrived(c, 4, blk_dp)
+            start(c, "dp")
+
+        @pl.when(ready)
+        def _():
+            piece(b, 3)
+            out_copy(b).start()
+
+        @pl.when(live)
+        def _():
+            arrived(c, 7, blk_fp)
+            start(c, "fp")
+
+    @pl.loop(0, chunks)
+    def _(c):
+        for name in ("own", "p", "u", "d", "f", "up", "dp", "fp"):
+            for one in sends(c, name):
+                one.wait_send()
+
+    for slot, (t, c) in enumerate(targets):
+
+        @pl.when((t != tm) | (c != me))
+        def _():
+            src_copy(t, c, slot % per, slot, me).wait_send()
+
+    out_copy(chunks - 2).wait()
+    out_copy(chunks - 1).wait()
+
+
+def corr(wh, own_src, n_tm, n_chan):
+    count, n = wh.shape
+    total = n * n_chan
+    chunks = count // COLS
+    dma = pltpu.SemaphoreType.DMA
+    flops = 2 * LAGS * 8 * count * total
     return pl.pallas_call(
         corr_kernel,
-        grid=(total_rec // cols,),
-        in_specs=[
-            pl.BlockSpec(src.shape, lambda i: (0, 0)),
-            pl.BlockSpec((cols, total), lambda i: (i, 0)),
+        in_specs=[pl.BlockSpec(memory_space=pl.ANY), pl.BlockSpec(memory_space=pltpu.VMEM)],
+        out_specs=pl.BlockSpec(memory_space=pl.ANY),
+        out_shape=jax.ShapeDtypeStruct((LAGS, 8, count), F32),
+        scratch_shapes=[
+            pltpu.VMEM((count, total), BF),
+            pltpu.VMEM(((LAGS + 1) * 8, total), BF),
+            pltpu.VMEM((8, total + 384), F32),
+            pltpu.VMEM((2, LAGS, 8, COLS), F32),
+            dma(()),
+            dma((16, chunks)),
+            dma((16, chunks)),
+            dma((16,)),
+            dma((n_chan,)),
+            dma((2,)),
         ],
-        out_specs=pl.BlockSpec((count, LAGS, cols), lambda i: (0, 0, i)),
-        out_shape=jax.ShapeDtypeStruct((count, LAGS, total_rec), F32),
-        scratch_shapes=[pltpu.VMEM((count * LPAD, total), BF)],
-        compiler_params=pltpu.CompilerParams(vmem_limit_bytes=56 << 20),
+        compiler_params=pltpu.CompilerParams(
+            collective_id=0, has_side_effects=True, vmem_limit_bytes=58 << 20
+        ),
+        cost_estimate=pl.CostEstimate(flops=flops, bytes_accessed=3 * count * total, transcendentals=0),
         name="corr",
-    )(src, rec)
-
-
-def lag_source(sources):
-    total = sources.shape[1]
-    left = 256 - HALF
-    return jnp.pad(sources, ((0, 0), (left, HALF))).astype(F32)
-
-
-def toeplitz(fir_taps):
-    diff = lax.broadcasted_iota(jnp.int32, (384, 256), 0) - lax.broadcasted_iota(jnp.int32, (384, 256), 1)
-    out = jnp.zeros((384, 256), F32)
-    for k in range(fir_taps.shape[0]):
-        out = jnp.where(diff == k, fir_taps[k], out)
-    return out
+    )(wh, own_src)
 
 
 def shards(raw_data, fir_taps, spectral_weight):
@@ -190,16 +413,13 @@
     ends = chan_count - 1
     left = lax.ppermute(raw_data[:, samples_dev - HALO :], "chan", [(i, i + 1) for i in range(ends)])
     right = lax.ppermute(raw_data[:, :HALO], "chan", [(i + 1, i) for i in range(ends)])
+    taps = jnp.pad(fir_taps, (0, 384 - fir_taps.shape[0]))[None, :]
     weight = jnp.concatenate([spectral_weight, spectral_weight])[None, :]
-    whitened = front(raw_data, left, right, toeplitz(fir_taps), weight)
-    source_dev = 128 // chan_count
+    whitened = front(raw_data, left, right, taps, weight)
     stride = channels_dev * tm_count // 128
-    own = whitened[::stride]
-    every = lax.all_gather(own, "chan", axis=1, tiled=True)
-    every = lax.all_gather(every, "tm", axis=0, tiled=True)
-    sources = lax.dynamic_slice_in_dim(every, lax.axis_index("chan") * source_dev, source_dev, 0)
-    receivers = lax.all_gather(whitened, "chan", axis=1, tiled=True)
-    return corr(lag_source(sources), receivers)
+    own = whitened[::stride].astype(F32)
+    result = corr(whitened, own, tm_count, chan_count)
+    return result.transpose(1, 0, 2)
 
 
 def solution(mesh):

time: 295 us -> 159 us (0.54)
  waiting for transfers between devices: 134 us -> 7.43 us
  Pallas kernels: 71.8 us -> 126 us
  blocking collectives: 22.5 us -> 0 us
  other arithmetic: 22.5 us -> 1.42 us
  between operations: 13.5 us -> 0.1 us
  local copies, waits for them, and re-layouts: 23.1 us -> 17.1 us
    all_gather x2 -> x0, waiting for transfers between devices: 134 us -> none  [the longest x1 86.1 us: shards(): receivers = lax.all_gather(whitened, 'chan', axis=1, tiled=True)]
    pallas_call x1, Pallas kernels: 57.8 us -> 113 us  [corr(): pl.pallas_call(corr_kernel, in_specs=[pl.BlockSpec(memory_space=pl.ANY),...]
    all_gather x1 -> x0, blocking collectives: 22.5 us -> none  [shards(): every = lax.all_gather(own, 'chan', axis=1, tiled=True)]
    select_n x1 -> x0, other arithmetic: 21.7 us -> none  [toeplitz(): out = jnp.where(diff == k, fir_taps[k], out)]
    pallas_call x1 -> x0, local copies, waits for them, and re-layouts: 11.5 us -> none  [corr(): pl.pallas_call(corr_kernel, grid=(total_rec // cols,), in_specs=[pl.Block...]
    unnamed x16 -> x13, local copies, waits for them, and re-layouts: 4.01 us -> 12.1 us
    ppermute x1, waiting for transfers between devices: 0.01 us -> 5.86 us  [shards(): lax.ppermute(raw_data[:, :HALO], 'chan', [(i + 1, i) for i in range(ends)])]
  transfers between devices with their start and end apart: 4 -> 2, of which waited for: 2 -> 2; matrix products, arithmetic and copies ran while one was open for 9% -> 1% of each run, Pallas kernels for 0% -> 0%
where the time goes in v1:
time: 159 us
  Pallas kernels  126 us (79%)
  local copies, waits for them, and re-layouts  17.1 us (11%)
  waiting for transfers between devices  7.43 us (5%)
  starting transfers between devices  6.42 us (4%)
    pallas_call x1, Pallas kernels, corr(): pl.pallas_call(corr_kernel, in_specs=[pl.BlockSpec(memory_space=pl.ANY),...  113 us
    pallas_call x1, Pallas kernels, front(): pl.pallas_call(front_kernel, grid=(count // rows,), in_specs=[blk(n), blk...  13.4 us
    unnamed x13, local copies, waits for them, and re-layouts  12.1 us
    ppermute x1, waiting for transfers between devices, shards(): lax.ppermute(raw_data[:, :HALO], 'chan', [(i + 1, i) for i in range(ends)])  5.86 us
    ppermute x1, starting transfers between devices, shards(): lax.ppermute(raw_data[:, samples_dev - HALO:], 'chan', [(i, i + 1) for i...  4.5 us
  transfers between devices with their start and end apart: 2, of which 2 were waited for; matrix products, arithmetic and copies ran while one was open for 1% of the time, Pallas kernels for 0%

profile of v1, /device:TPU:1, one launch (start us, length us, event | category | flops | bytes accessed | tf_op | source)
XLA Modules:
  0.0 158.7 jit_solution(8878828900994934193)
XLA Ops:
  0.0 0.0 copy-start
  0.0 1.7 %fusion = (f32[1280,80]{1,0:T(8,128)S(1)}, f32[1280,80]{1,0:T(8,128)S(1)}) fusion(f32[1280,384]{1,0:T(8,128)} %raw.1), kind=kLoop, calls=%fused_computation.1 | loop fusion | bytes 1638400 | tf_op jit(solution)/shard_map/slice | solution.py:415
  1.7 1.0 copy.12
  2.7 4.5 %collective-permute-start = (f32[1280,80]{0,1:T(8,128)}, f32[1280,80]{0,1:T(8,128)S(1)}, u32[]{:S(2)}, u32[]{:S(2)}) collective-permute-start(f32[1280,80]{0,1:T(8,128)} %copy.12), channel_id=1, source_target_pairs={{0,1},{1,2},{2,3},{3,4},{4,5},{5,6},{6,7},{7,8},{8,9},{9,10},{10,1... | collective-permute-start | bytes 1228808 | tf_op jit(solution)/shard_map/ppermute | solution.py:414
  7.2 0.2 copy.13
  7.4 1.9 %collective-permute-start.1 = (f32[1280,80]{0,1:T(8,128)S(1)}, f32[1280,80]{0,1:T(8,128)}, u32[]{:S(2)}, u32[]{:S(2)}) collective-permute-start(f32[1280,80]{0,1:T(8,128)S(1)} %copy.13), channel_id=1, source_target_pairs={{1,0},{2,1},{3,2},{4,3},{5,4},{6,5},{7,6},{8,7},{9,8},{10,9},{11,1... | collective-permute-start | bytes 1228808 | tf_op jit(solution)/shard_map/ppermute | solution.py:415
  9.3 0.7 pad.4
  10.0 0.8 maximum_bitcast_fusion.weight
  10.8 1.6 collective-permute-done
  12.3 0.2 copy.10.left
  12.6 5.9 %collective-permute-done.1 = f32[1280,80]{0,1:T(8,128)} collective-permute-done((f32[1280,80]{0,1:T(8,128)S(1)}, f32[1280,80]{0,1:T(8,128)}, u32[]{:S(2)}, u32[]{:S(2)}) %collective-permute-start.1) | collective-permute-done | bytes 409632 | tf_op jit(solution)/shard_map/ppermute | solution.py:415
  18.4 1.2 copy.11.right
  19.7 0.0 copy-done
  19.7 0.0 copy-start.2
  19.7 0.9 copy-done.2
  20.6 0.0 copy-start.3
  20.6 0.9 copy-done.3
  21.5 0.0 copy-start.4
  21.5 0.9 copy-done.4
  22.4 13.4 %front.1.wh = bf16[1280,384]{1,0:T(8,128)(2,1)S(1)} custom-call(f32[1280,384]{1,0:T(8,128)S(1)} %copy-done, f32[1280,80]{1,0:T(8,128)S(1)} %copy.10.left, f32[1280,80]{1,0:T(8,128)S(1)} %copy.11.right, f32[1,384]{1,0:T(1,128)S(1)} %broadcast_in_dim.6.toep, f32[1,128]{1,0:T(1,128)S(1)} %maximum_bitcast_fusion.weight, bf16[256,256]{1,0:T(8,128)(2,1)S(1)} %copy-done.4, ...), custom_call_target="tpu_custom_call" | custom-call | tf_op jit(solution)/shard_map/front/pallas_call | solution.py:111
  35.9 0.0 copy-start.1
  35.9 0.9 copy-done.1
  36.8 1.2 slice.11
  38.1 0.6 convert_element_type.5.own_src
  38.7 112.8 %corr.1 = f32[201,8,1280]{2,1,0:T(8,128)} custom-call(bf16[1280,384]{1,0:T(8,128)(2,1)} %copy-done.1, f32[16,384]{1,0:T(8,128)} %convert_element_type.5.own_src), custom_call_target="tpu_custom_call" | custom-call | flops 25291653120 | bytes 23592960 | tf_op jit(solution)/shard_map/corr/pallas_call | solution.py:384
  151.5 7.2 %copy.15 = f32[8,201,1280]{2,0,1:T(8,128)} copy(f32[8,201,1280]{2,0,1:T(8,128)} %bitcast.3) | data formatting | bytes 16465920
  (2 shorter events, 0.0 us)
Async XLA Ops:
  0.0 19.7 %copy-start = (f32[1280,384]{1,0:T(8,128)S(1)}, f32[1280,384]{1,0:T(8,128)}, u32[]{:S(2)}) copy-start(f32[1280,384]{1,0:T(8,128)} %raw.1) | copy-start | bytes 5898244
  2.7 9.7 %collective-permute-start = (f32[1280,80]{0,1:T(8,128)}, f32[1280,80]{0,1:T(8,128)S(1)}, u32[]{:S(2)}, u32[]{:S(2)}) collective-permute-start(f32[1280,80]{0,1:T(8,128)} %copy.12), channel_id=1, source_target_pairs={{0,1},{1,2},{2,3},{3,4},{4,5},{5,6},{6,7},{7,8},{8,9},{9,10},{10,1... | collective-permute-start | bytes 1228808 | tf_op jit(solution)/shard_map/ppermute | solution.py:414
  7.4 11.1 %collective-permute-start.1 = (f32[1280,80]{0,1:T(8,128)S(1)}, f32[1280,80]{0,1:T(8,128)}, u32[]{:S(2)}, u32[]{:S(2)}) collective-permute-start(f32[1280,80]{0,1:T(8,128)S(1)} %copy.13), channel_id=1, source_target_pairs={{1,0},{2,1},{3,2},{4,3},{5,4},{6,5},{7,6},{8,7},{9,8},{10,9},{11,1... | collective-permute-start | bytes 1228808 | tf_op jit(solution)/shard_map/ppermute | solution.py:415
  19.7 0.9 copy-start.2
  20.6 0.9 copy-start.3
  21.5 0.9 copy-start.4
  35.9 0.9 copy-start.1

commit v2 on v1

v2 whole, which is shorter than its diff:
```python
import jax
import jax.numpy as jnp
import ml_dtypes
import numpy as np
from jax import lax
from jax.experimental import pallas as pl
from jax.experimental.pallas import tpu as pltpu
from jax.sharding import PartitionSpec as P

HK = 16
TN = 64
SEG = 128
HALF = 100
LAGS = 201
EPS = 1e-06
FLOOR = 0.5
HALO = HK + TN
BF = jnp.bfloat16
F32 = jnp.float32


def split_np(table):
    table = np.asarray(table, np.float32)
    hi = table.astype(ml_dtypes.bfloat16)
    lo = (table - hi.astype(np.float32)).astype(ml_dtypes.bfloat16)
    return hi, lo


def tables():
    t, f = np.arange(SEG), np.arange(SEG // 2)
    angle = 2.0 * np.pi * ((t[:, None] * f[None, :]) % SEG) / SEG
    forward = np.concatenate([np.cos(angle), np.sin(angle)], axis=1)
    weight = np.where(f == 0, 1.0, 2.0)[:, None]
    inverse = np.concatenate([np.cos(angle).T * weight, np.sin(angle).T * weight]) / np.sqrt(SEG)
    stacked = []
    for table in (forward, inverse):
        row = np.concatenate(split_np(table), axis=1)
        stacked.append(np.concatenate([row, row], axis=0))
    i, o = np.arange(384)[:, None], np.arange(256)[None, :]
    band = ((i - o >= 0) & (i - o <= 2 * TN)).astype(ml_dtypes.bfloat16)
    mean = np.full((256, 128), 1.0 / 128, ml_dtypes.bfloat16)
    return stacked[0], stacked[1], band, mean


def dot(a, b):
    return jnp.dot(a, b, preferred_element_type=F32)


def split2(x):
    hi = x.astype(BF)
    return hi, (x - hi.astype(F32)).astype(BF)


def split3(x):
    hi = x.astype(BF)
    rest = x - hi.astype(F32)
    mid = rest.astype(BF)
    return hi, mid, (rest - mid.astype(F32)).astype(BF)


def whiten_rows(left, raw, right, ext, taps, weight, fwd, inv, band, mean):
    rows, n = raw.shape
    here = pl.ds(0, rows)
    chan, ends = lax.axis_index("chan"), lax.axis_size("chan") - 1
    ext[here, 0:HALO] = left[:, left.shape[1] - HALO :]
    ext[here, HALO : HALO + n] = raw
    ext[here, HALO + n : 2 * HALO + n] = right[:, :HALO]
    t_hi, t_mid, t_lo = taps

    def fir(x):
        hi, mid, lo = split3(x)
        small = dot(mid, t_mid[...]) + dot(hi, t_lo[...]) + dot(lo, t_hi[...])
        return (small + (dot(hi, t_mid[...]) + dot(mid, t_hi[...]))) + dot(hi, t_hi[...])

    f = jnp.concatenate([fir(ext[here, 0:384]), fir(ext[here, 256:640])], axis=1)
    lane = lax.broadcasted_iota(jnp.int32, (1, 512), 1)
    low = jnp.where(chan == 0, TN, 0)
    high = jnp.where(chan == ends, TN + n, 512)
    f = jnp.where((lane >= low) & (lane < high), f, 0.0)
    hi, lo = split2(jnp.abs(f))
    first = dot(hi[:, 0:384], band[...]) + dot(lo[:, 0:384], band[...])
    second = dot(hi[:, 256:512], band[0:256, 0:128]) + dot(lo[:, 256:512], band[0:256, 0:128])
    summed = jnp.concatenate([first, second], axis=1)
    norm = f[:, TN : TN + n] / (summed * (1.0 / (2 * TN + 1)) + EPS)
    parts = []
    for s in range(n // SEG):
        x = norm[:, s * SEG : (s + 1) * SEG]
        p = dot(jnp.concatenate(split2(x), axis=1), fwd[...])
        spec = p[:, :SEG] + p[:, SEG:]
        sq = spec * spec
        amp = jnp.sqrt(sq + pltpu.roll(sq, SEG // 2, 1))
        mean_amp = dot(jnp.concatenate(split2(amp), axis=1), mean[...]) + EPS
        z = spec * (weight[...] / jnp.maximum(amp, FLOOR * mean_amp))
        q = dot(jnp.concatenate(split2(z), axis=1), inv[...])
        parts.append((q[:, :SEG] + q[:, SEG:]).astype(BF))
    return jnp.concatenate(parts, axis=1)


AHEAD = 4
HALOS_AHEAD = 7
LANES = 128
COLS = 256
ROWS = 128
PIECES = 4


def build_lags(z, lagged, total, part, parts):
    lane = lax.broadcasted_iota(jnp.int32, (8, 128), 1)
    blocks = total // 128

    @pl.loop(part * (64 // parts), (part + 1) * (64 // parts))
    def _(p):
        shift = p * 2
        tiles = []
        for one in (shift, shift + 1):
            rolled = [pltpu.roll(z[:, j * 128 : (j + 1) * 128], one, 1) for j in range(1, blocks + 3)]
            tiles.append([jnp.where(lane < one, rolled[j], rolled[j + 1]) for j in range(blocks + 1)])
        pairs = [jnp.concatenate([tiles[0][j], tiles[1][j]], axis=0).astype(BF) for j in range(blocks + 1)]

        @pl.when(shift + HALF < LAGS)
        def _():
            row = pl.ds(pl.multiple_of((shift + HALF) * 8, 16), 16)
            for j in range(blocks):
                lagged[row, j * 128 : (j + 1) * 128] = pairs[j]

        @pl.when(shift >= 128 - HALF)
        def _():
            row = pl.ds(pl.multiple_of((shift - (128 - HALF)) * 8, 16), 16)
            for j in range(blocks):
                lagged[row, j * 128 : (j + 1) * 128] = pairs[j + 1]


def corr_kernel(
    raw_hbm, taps, weight, fwd, inv, band, mean, out,
    rec, lagged, z, stage, raw, wh, own_src, ext, left, right, few, few_left, few_right, t_hi, t_mid, t_lo,
    raw_sem, own_sem, send, recv, src_send, src_recv, out_sem, halo_send, halo_recv,
):
    tm, me = lax.axis_index("tm"), lax.axis_index("chan")
    n_tm, n_chan = lax.axis_size("tm"), lax.axis_size("chan")
    count, n = wh.shape
    total = n * n_chan
    chunks, steps = count // COLS, count // ROWS
    y, x, core = me // 4, (me // 2) % 2, me % 2
    n_y = n_chan // 4
    up, down, far = (y + 1) % n_y, (y + n_y - 1) % n_y, (y + 2) % n_y

    def at(yy, xx, cc):
        return (yy * 2 + xx) * 2 + cc

    raw_copy = pltpu.make_async_copy(raw_hbm, raw, raw_sem)
    raw_copy.start()
    to_x, to_u, to_d, to_s = at(y, 1 - x, core), at(up, x, core), at(down, x, core), at(y, x, 1 - core)

    def lanes(b):
        return pl.ds(pl.multiple_of(b * n, 128), n)

    def signal(t, c):
        pl.semaphore_signal(
            pltpu.get_barrier_semaphore(), inc=1, device_id=(t, c), device_id_type=pl.DeviceIdType.MESH
        )

    per = n_chan // n_tm
    targets = [(t, per * tm + h) for t in range(n_tm) for h in range(per)]
    origins = [(me // per, c) for c in range(n_chan)]
    for t, c in targets + origins:

        @pl.when((t != tm) | (c != me))
        def _():
            signal(t, c)

    before, after = (me + n_chan - 1) % n_chan, (me + 1) % n_chan
    for c in (to_x, to_u, to_d, to_s, before, after):
        signal(tm, c)
    barrier = pltpu.get_barrier_semaphore()
    mine = me // per == tm

    @pl.when(mine)
    def _():
        pl.semaphore_wait(barrier, len(targets) + len(origins) + 4)

    @pl.when(jnp.logical_not(mine))
    def _():
        pl.semaphore_wait(barrier, len(targets) + len(origins) + 6)

    def src_copy(t, c, h, send_slot, who):
        return pltpu.make_async_remote_copy(
            src_ref=own_src.at[h * 8 : (h + 1) * 8, :],
            dst_ref=z.at[:, pl.ds(pl.multiple_of(256 + who * n, 128), n)],
            send_sem=src_send.at[send_slot],
            recv_sem=src_recv.at[who],
            device_id=(t, c),
            device_id_type=pl.DeviceIdType.MESH,
        )

    def copy(s_kind, r_kind, c, target, block, half=None, source=None):
        size = ROWS if half is None else ROWS // 2
        start = c * ROWS + (0 if half is None else half * size)
        rows = pl.ds(pl.multiple_of(start, ROWS // 2), size)
        return pltpu.make_async_remote_copy(
            src_ref=rec.at[rows, lanes(block)] if source is None else source.at[rows, :],
            dst_ref=rec.at[rows, lanes(block)],
            send_sem=send.at[s_kind, c],
            recv_sem=recv.at[r_kind, c],
            device_id=(tm, target),
            device_id_type=pl.DeviceIdType.MESH,
        )

    blk_p, blk_u, blk_d = at(y, 1 - x, core), at(up, x, core), at(down, x, core)
    blk_up, blk_dp = at(up, 1 - x, core), at(down, 1 - x, core)
    blk_f, blk_fp = at(far, x, core), at(far, 1 - x, core)

    def sends(c, name):
        table = {
            "own": [
                (0, 0, c, to_x, me, None, wh),
                (1, 2, c, to_u, me, None, wh),
                (2, 1, c, to_d, me, None, wh),
                (3, 8, c, to_s, me, None, wh),
            ],
            "p": [(4, 4, c, to_u, blk_p), (5, 3, c, to_d, blk_p), (6, 9, c, to_s, blk_p)],
            "u": [(7, 6, c, to_d, blk_u, 1), (8, 10, c, to_s, blk_u)],
            "d": [(9, 5, c, to_u, blk_d, 0), (10, 11, c, to_s, blk_d)],
            "f": [(11, 7, c, to_x, blk_f), (12, 14, c, to_s, blk_f)],
            "up": [(13, 12, c, to_s, blk_up)],
            "dp": [(14, 13, c, to_s, blk_dp)],
            "fp": [(15, 15, c, to_s, blk_fp)],
        }
        return [copy(*one) for one in table[name]]

    def start(c, *names):
        for name in names:
            for one in sends(c, name):
                one.start()

    def arrived(c, r_kind, block, half=None):
        copy(0, r_kind, c, to_x, block, half=half).wait_recv()

    tables = ((t_hi, t_mid, t_lo), weight, fwd, inv, band, mean)
    has_left, has_right = me > 0, me < n_chan - 1
    last_lanes, first_lanes = pl.ds(n - LANES, LANES), pl.ds(0, LANES)

    def halo_to_right(source, target, c):
        return pltpu.make_async_remote_copy(
            src_ref=source, dst_ref=target, send_sem=halo_send.at[0, c], recv_sem=halo_recv.at[0, c],
            device_id=(tm, after), device_id_type=pl.DeviceIdType.MESH,
        )

    def halo_to_left(source, target, c):
        return pltpu.make_async_remote_copy(
            src_ref=source, dst_ref=target, send_sem=halo_send.at[1, c], recv_sem=halo_recv.at[1, c],
            device_id=(tm, before), device_id_type=pl.DeviceIdType.MESH,
        )

    def step_rows(c):
        return pl.ds(pl.multiple_of(c * ROWS, ROWS), ROWS)

    def halo_pair(c):
        rows = step_rows(c)
        return (
            halo_to_right(raw.at[rows, last_lanes], left.at[rows, :], c),
            halo_to_left(raw.at[rows, first_lanes], right.at[rows, :], c),
        )

    few_pair = (
        halo_to_right(few.at[:, last_lanes], few_left, steps),
        halo_to_left(few.at[:, first_lanes], few_right, steps),
    )

    def on_sides(pair, name, flip=False):
        sides = (has_left, has_right) if flip else (has_right, has_left)
        for one, there in zip(pair, sides):
            pl.when(there)(getattr(one, name))

    def own_copy(c):
        return pltpu.make_async_copy(wh.at[step_rows(c), :], rec.at[step_rows(c), lanes(me)], own_sem.at[c])

    def whiten_step(c):
        rows = step_rows(c)
        on_sides(halo_pair(c), "wait_recv", flip=True)
        wh[rows, :] = whiten_rows(left[rows, :], raw[rows, :], right[rows, :], ext, *tables)
        start(c, "own")
        own_copy(c).start()

    raw_copy.wait()
    stride = count * n_tm // (8 * n_chan)
    for k in range(8 * per):
        few[k : k + 1, :] = raw[k * stride : k * stride + 1, :]
    on_sides(few_pair, "start")
    for c in range(min(HALOS_AHEAD, steps)):
        on_sides(halo_pair(c), "start")

    @pl.when(me == 0)
    def _():
        left[...] = jnp.zeros(left.shape, F32)
        few_left[...] = jnp.zeros(few_left.shape, F32)

    @pl.when(me == n_chan - 1)
    def _():
        right[...] = jnp.zeros(right.shape, F32)
        few_right[...] = jnp.zeros(few_right.shape, F32)

    rolled = pltpu.roll(jnp.broadcast_to(taps[...], (256, 384)), 0, 1, stride=1, stride_axis=0)
    hi, mid, lo = split3(rolled.T)
    t_hi[...] = hi
    t_mid[...] = mid
    t_lo[...] = lo
    ext[...] = jnp.zeros(ext.shape, F32)
    z[:, 0:256] = jnp.zeros((8, 256), F32)
    z[:, 256 + total :] = jnp.zeros((8, 128), F32)
    on_sides(few_pair, "wait_recv", flip=True)
    own_src[...] = whiten_rows(few_left[...], few[...], few_right[...], ext, *tables).astype(F32)

    for slot, (t, c) in enumerate(targets):

        @pl.when((t != tm) | (c != me))
        def _():
            src_copy(t, c, slot % per, slot, me).start()

    @pl.when(mine)
    def _():
        z[:, pl.ds(pl.multiple_of(256 + me * n, 128), n)] = own_src[pl.ds(pl.multiple_of((me % per) * 8, 8), 8), :]

    @pl.loop(0, min(AHEAD, steps))
    def _(c):
        whiten_step(c)

    def lag_part(part, parts):
        @pl.when(part == 0)
        def _():
            for c in range(n_chan):

                @pl.when((me // per != tm) | (c != me))
                def _():
                    src_copy(tm, to_x, 0, 0, c).wait_recv()

        build_lags(z, lagged, total, part, parts)

    scale = total**-0.5
    used = LAGS * 8
    step = -(-used // PIECES // 16) * 16

    def out_copy(c):
        return pltpu.make_async_copy(
            stage.at[c % 2], out.at[:, :, pl.ds(pl.multiple_of(c * COLS, 128), COLS)], out_sem.at[c % 2]
        )

    def piece(c, i):
        first = i * step
        rows = min(step, used - first)
        full = -(-rows // 16) * 16
        acc = lax.dot_general(
            lagged[first : first + full, :],
            rec[pl.ds(pl.multiple_of(c * COLS, 128), COLS), :],
            (((1,), (1,)), ((), ())),
            preferred_element_type=F32,
        )
        stage[c % 2, first // 8 : (first + rows) // 8] = (acc[:rows] * scale).reshape(rows // 8, 8, COLS)

    def near(c):
        @pl.when(c < steps)
        def _():
            @pl.when(c + HALOS_AHEAD < steps)
            def _():
                on_sides(halo_pair(c + HALOS_AHEAD), "start")

            @pl.when(c + AHEAD < steps)
            def _():
                whiten_step(c + AHEAD)

            arrived(c, 0, blk_p)
            start(c, "p")

    def ring(c):
        @pl.when(c < steps)
        def _():
            arrived(c, 1, blk_u)
            start(c, "u")
            arrived(c, 2, blk_d)
            start(c, "d")

        @pl.when((c >= 1) & (c <= steps))
        def _():
            arrived(c - 1, 5, blk_f, half=0)
            arrived(c - 1, 6, blk_f, half=1)
            start(c - 1, "f")

    def last(c):
        @pl.when((c >= 1) & (c <= steps))
        def _():
            arrived(c - 1, 3, blk_up)
            start(c - 1, "up")
            arrived(c - 1, 4, blk_dp)
            start(c - 1, "dp")

        @pl.when((c >= 2) & (c <= steps + 1))
        def _():
            arrived(c - 2, 7, blk_fp)
            start(c - 2, "fp")

    def twin(c):
        for kind, yy in ((8, y), (9, y), (10, up), (11, down), (12, up), (13, down), (14, far), (15, far)):
            xx = x if kind in (8, 10, 11, 14) else 1 - x
            arrived(c, kind, at(yy, xx, 1 - core))

    @pl.loop(0, chunks + 2)
    def _(m):
        b = m - 2
        ready = b >= 0

        near(2 * m)

        @pl.when(m < 2)
        def _():
            lag_part(2 * m, 4)

        @pl.when(ready)
        def _():
            for c in (2 * b, 2 * b + 1):
                twin(c)
                own_copy(c).wait()

            @pl.when(b >= 2)
            def _():
                out_copy(b - 2).wait()

            piece(b, 0)

        ring(2 * m)

        @pl.when(ready)
        def _():
            piece(b, 1)

        last(2 * m)
        near(2 * m + 1)

        @pl.when(m < 2)
        def _():
            lag_part(2 * m + 1, 4)

        @pl.when(ready)
        def _():
            piece(b, 2)

        ring(2 * m + 1)

        @pl.when(ready)
        def _():
            piece(b, 3)
            out_copy(b).start()

        last(2 * m + 1)

    @pl.loop(0, steps)
    def _(c):
        for name in ("own", "p", "u", "d", "f", "up", "dp", "fp"):
            for one in sends(c, name):
                one.wait_send()

        on_sides(halo_pair(c), "wait_send")

    on_sides(few_pair, "wait_send")
    for slot, (t, c) in enumerate(targets):

        @pl.when((t != tm) | (c != me))
        def _():
            src_copy(t, c, slot % per, slot, me).wait_send()

    out_copy(chunks - 2).wait()
    out_copy(chunks - 1).wait()


def shards(raw_data, fir_taps, spectral_weight):
    count, n = raw_data.shape
    n_tm, n_chan = lax.axis_size("tm"), lax.axis_size("chan")
    total = n * n_chan
    steps = count // ROWS
    few = 8 * n_chan // n_tm
    taps = jnp.pad(fir_taps, (0, 384 - fir_taps.shape[0]))[None, :]
    weight = jnp.concatenate([spectral_weight, spectral_weight])[None, :]
    consts = [jnp.asarray(t) for t in tables()]
    dma = pltpu.SemaphoreType.DMA
    vmem = pl.BlockSpec(memory_space=pltpu.VMEM)
    hbm = pl.BlockSpec(memory_space=pl.ANY)
    result = pl.pallas_call(
        corr_kernel,
        in_specs=[hbm] + [vmem] * 6,
        out_specs=hbm,
        out_shape=jax.ShapeDtypeStruct((LAGS, 8, count), F32),
        scratch_shapes=[
            pltpu.VMEM((count, total), BF),
            pltpu.VMEM(((LAGS + 1) * 8, total), BF),
            pltpu.VMEM((8, total + 384), F32),
            pltpu.VMEM((2, LAGS, 8, COLS), F32),
            pltpu.VMEM((count, n), F32),
            pltpu.VMEM((count, n), BF),
            pltpu.VMEM((few, n), F32),
            pltpu.VMEM((ROWS, 640), F32),
            pltpu.VMEM((count, LANES), F32),
            pltpu.VMEM((count, LANES), F32),
            pltpu.VMEM((few, n), F32),
            pltpu.VMEM((few, LANES), F32),
            pltpu.VMEM((few, LANES), F32),
            pltpu.VMEM((384, 256), BF),
            pltpu.VMEM((384, 256), BF),
            pltpu.VMEM((384, 256), BF),
            dma(()),
            dma((steps,)),
            dma((16, steps)),
            dma((16, steps)),
            dma((n_tm * (n_chan // n_tm),)),
            dma((n_chan,)),
            dma((2,)),
            dma((2, steps + 1)),
            dma((2, steps + 1)),
        ],
        compiler_params=pltpu.CompilerParams(
            collective_id=0, has_side_effects=True, vmem_limit_bytes=60 << 20
        ),
        name="corr",
    )(raw_data, taps, weight, *consts)
    return result.transpose(1, 0, 2)


def solution(mesh):
    in_specs = (P("tm", "chan"), P(), P())
    out_specs = P("chan", None, "tm")
    return jax.shard_map(shards, mesh=mesh, in_specs=in_specs, out_specs=out_specs, check_vma=False)
```

time: 159 us -> 112 us (0.70)
  Pallas kernels: 126 us -> 101 us
  local copies, waits for them, and re-layouts: 17.1 us -> 9.03 us
  waiting for transfers between devices: 7.43 us -> 0 us
  starting transfers between devices: 6.42 us -> 0 us
    pallas_call x2 -> x1, Pallas kernels: 126 us -> 101 us  [shards(): pl.pallas_call(corr_kernel, in_specs=[hbm] + [vmem] * 6, out_specs=hbm, o...]
    ppermute x2 -> x0, waiting for transfers between devices: 7.43 us -> none  [the longest x1 5.86 us: shards(): lax.ppermute(raw_data[:, :HALO], 'chan', [(i + 1, i) for i in range(ends)])]
    ppermute x2 -> x0, starting transfers between devices: 6.42 us -> none  [the longest x1 4.5 us: shards(): lax.ppermute(raw_data[:, samples_dev - HALO:], 'chan', [(i, i + 1) for i...]
    unnamed x13 -> x1, local copies, waits for them, and re-layouts: 12.1 us -> 7.21 us
    slice x2 -> x0, local copies, waits for them, and re-layouts: 2.91 us -> none  [the longest x1 1.67 us: shards(): raw_data[:, :HALO]]
  transfers between devices with their start and end apart: 2 -> 0, of which waited for: 2 -> 0; matrix products, arithmetic and copies ran while one was open for 1% -> 0% of each run, Pallas kernels for 0% -> 0%
where the time goes in v2:
time: 112 us
  Pallas kernels  101 us (90%)
  local copies, waits for them, and re-layouts  9.03 us (8%)
  other arithmetic  1.3 us (1%)
    pallas_call x1, Pallas kernels, shards(): pl.pallas_call(corr_kernel, in_specs=[hbm] + [vmem] * 6, out_specs=hbm, o...  101 us
    unnamed x1, local copies, waits for them, and re-layouts  7.21 us

profile of v2, /device:TPU:1, one launch (start us, length us, event | category | flops | bytes accessed | tf_op | source)
XLA Modules:
  0.0 111.7 jit_solution(13435436825203418151)
XLA Ops:
  0.0 1.3 %maximum_bitcast_fusion.weight = f32[1,128]{1,0:T(1,128)} fusion(f32[64]{0:T(128)} %param.9), kind=kLoop, calls=%fused_computation | loop fusion | flops 128 | bytes 768 | tf_op jit(solution)/shard_map/broadcast_in_dim | solution.py:480
  1.3 0.7 pad.4
  2.0 0.5 broadcast_in_dim.6.taps
  2.5 0.6 jit_solution_.3.mean
  3.1 101.3 %corr.1 = f32[201,8,1280]{2,1,0:T(8,128)} custom-call(f32[1280,384]{1,0:T(8,128)} %raw_hbm.1, f32[1,384]{1,0:T(1,128)} %broadcast_in_dim.6.taps, f32[1,128]{1,0:T(1,128)} %maximum_bitcast_fusion.weight, bf16[256,256]{1,0:T(8,128)(2,1)} %constant.11.clone.fwd, bf16[256,256]{1,0:T(8,128)(2,1)} %constant.12.clone.inv, bf16[384,256]{1,0:T(8,128)(2,1)} %constant.13.clone.band, ...), custom_call_target="tpu_custom_call" | custom-call | tf_op jit(solution)/shard_map/corr/pallas_call | solution.py:485
  104.5 7.2 %copy.9 = f32[8,201,1280]{2,0,1:T(8,128)} copy(f32[8,201,1280]{2,0,1:T(8,128)} %bitcast.3) | data formatting | bytes 16465920

commit v3 on v2

--- a/solution.py
+++ b/solution.py
@@ -38,8 +38,7 @@
         stacked.append(np.concatenate([row, row], axis=0))
     i, o = np.arange(384)[:, None], np.arange(256)[None, :]
     band = ((i - o >= 0) & (i - o <= 2 * TN)).astype(ml_dtypes.bfloat16)
-    mean = np.full((256, 128), 1.0 / 128, ml_dtypes.bfloat16)
-    return stacked[0], stacked[1], band, mean
+    return stacked[0], stacked[1], band
 
 
 def dot(a, b):
@@ -131,8 +130,8 @@
 
 
 def corr_kernel(
-    raw_hbm, taps, weight, fwd, inv, band, mean, out,
-    rec, lagged, z, stage, raw, wh, own_src, ext, left, right, few, few_left, few_right, t_hi, t_mid, t_lo,
+    raw_hbm, taps, spectral, fwd, inv, band, out,
+    rec, lagged, z, stage, raw, wh, own_src, ext, left, right, few, few_left, few_right, t_hi, t_mid, t_lo, weight, mean,
     raw_sem, own_sem, send, recv, src_send, src_recv, out_sem, halo_send, halo_recv,
 ):
     tm, me = lax.axis_index("tm"), lax.axis_index("chan")
@@ -299,7 +298,13 @@
         right[...] = jnp.zeros(right.shape, F32)
         few_right[...] = jnp.zeros(few_right.shape, F32)
 
-    rolled = pltpu.roll(jnp.broadcast_to(taps[...], (256, 384)), 0, 1, stride=1, stride_axis=0)
+    bins = spectral.shape[1]
+    weight[:, :bins] = spectral[...]
+    weight[:, bins:] = spectral[...]
+    mean[...] = jnp.full(mean.shape, 1.0 / (2 * bins), BF)
+    ext[0:8, :] = jnp.zeros((8, ext.shape[1]), F32)
+    ext[0:1, 0 : taps.shape[1]] = taps[...]
+    rolled = pltpu.roll(jnp.broadcast_to(ext[0:1, 0:384], (256, 384)), 0, 1, stride=1, stride_axis=0)
     hi, mid, lo = split3(rolled.T)
     t_hi[...] = hi
     t_mid[...] = mid
@@ -344,17 +349,29 @@
             stage.at[c % 2], out.at[:, :, pl.ds(pl.multiple_of(c * COLS, 128), COLS)], out_sem.at[c % 2]
         )
 
-    def piece(c, i):
+    def partial(c, i, groups):
         first = i * step
         rows = min(step, used - first)
         full = -(-rows // 16) * 16
-        acc = lax.dot_general(
-            lagged[first : first + full, :],
-            rec[pl.ds(pl.multiple_of(c * COLS, 128), COLS), :],
-            (((1,), (1,)), ((), ())),
-            preferred_element_type=F32,
-        )
-        stage[c % 2, first // 8 : (first + rows) // 8] = (acc[:rows] * scale).reshape(rows // 8, 8, COLS)
+        acc = None
+        for group in groups:
+            span = pl.ds(pl.multiple_of(group * (4 * n), 128), 4 * n)
+            term = lax.dot_general(
+                lagged[first : first + full, span],
+                rec[pl.ds(pl.multiple_of(c * COLS, 128), COLS), span],
+                (((1,), (1,)), ((), ())),
+                preferred_element_type=F32,
+            )
+            acc = term if acc is None else acc + term
+        return slice(first // 8, (first + rows) // 8), acc[:rows].reshape(rows // 8, 8, COLS)
+
+    def near_piece(c, i):
+        where, acc = partial(c, i, (y, up, down))
+        stage[c % 2, where] = acc
+
+    def far_piece(c, i):
+        where, acc = partial(c, i, (far,))
+        stage[c % 2, where] = (stage[c % 2, where] + acc) * scale
 
     def near(c):
         @pl.when(c < steps)
@@ -397,57 +414,60 @@
             arrived(c - 2, 7, blk_fp)
             start(c - 2, "fp")
 
-    def twin(c):
-        for kind, yy in ((8, y), (9, y), (10, up), (11, down), (12, up), (13, down), (14, far), (15, far)):
+    def twin(c, kinds):
+        for kind in kinds:
+            yy = {8: y, 9: y, 10: up, 11: down, 12: up, 13: down, 14: far, 15: far}[kind]
             xx = x if kind in (8, 10, 11, 14) else 1 - x
             arrived(c, kind, at(yy, xx, 1 - core))
 
     @pl.loop(0, chunks + 2)
     def _(m):
-        b = m - 2
-        ready = b >= 0
-
         near(2 * m)
 
         @pl.when(m < 2)
         def _():
             lag_part(2 * m, 4)
 
+        ring(2 * m)
+
+        @pl.when(m >= 2)
+        def _():
+            b = m - 2
+            twin(2 * b, (14, 15))
+            twin(2 * b + 1, (14, 15))
+            for i in range(PIECES):
+                far_piece(b, i)
+            out_copy(b).start()
+
+        last(2 * m)
+        near(2 * m + 1)
+
+        @pl.when(m < 2)
+        def _():
+            lag_part(2 * m + 1, 4)
+
+        ready = (m >= 1) & (m <= chunks)
+
         @pl.when(ready)
         def _():
+            b = m - 1
             for c in (2 * b, 2 * b + 1):
-                twin(c)
+                twin(c, (8, 9, 10, 11, 12, 13))
                 own_copy(c).wait()
 
             @pl.when(b >= 2)
             def _():
                 out_copy(b - 2).wait()
 
-            piece(b, 0)
-
-        ring(2 * m)
+            near_piece(b, 0)
+            near_piece(b, 1)
+
+        ring(2 * m + 1)
 
         @pl.when(ready)
         def _():
-            piece(b, 1)
-
-        last(2 * m)
-        near(2 * m + 1)
-
-        @pl.when(m < 2)
-        def _():
-            lag_part(2 * m + 1, 4)
-
-        @pl.when(ready)
-        def _():
-            piece(b, 2)
-
-        ring(2 * m + 1)
-
-        @pl.when(ready)
-        def _():
-            piece(b, 3)
-            out_copy(b).start()
+            near_piece(m - 1, 2)
+            near_piece(m - 1, 3)
 
         last(2 * m + 1)
 
@@ -476,15 +496,13 @@
     total = n * n_chan
     steps = count // ROWS
     few = 8 * n_chan // n_tm
-    taps = jnp.pad(fir_taps, (0, 384 - fir_taps.shape[0]))[None, :]
-    weight = jnp.concatenate([spectral_weight, spectral_weight])[None, :]
     consts = [jnp.asarray(t) for t in tables()]
     dma = pltpu.SemaphoreType.DMA
     vmem = pl.BlockSpec(memory_space=pltpu.VMEM)
     hbm = pl.BlockSpec(memory_space=pl.ANY)
     result = pl.pallas_call(
         corr_kernel,
-        in_specs=[hbm] + [vmem] * 6,
+        in_specs=[hbm] + [vmem] * 5,
         out_specs=hbm,
         out_shape=jax.ShapeDtypeStruct((LAGS, 8, count), F32),
         scratch_shapes=[
@@ -504,6 +522,8 @@
             pltpu.VMEM((384, 256), BF),
             pltpu.VMEM((384, 256), BF),
             pltpu.VMEM((384, 256), BF),
+            pltpu.VMEM((1, SEG), F32),
+            pltpu.VMEM((256, SEG), BF),
             dma(()),
             dma((steps,)),
             dma((16, steps)),
@@ -518,7 +538,7 @@
             collective_id=0, has_side_effects=True, vmem_limit_bytes=60 << 20
         ),
         name="corr",
-    )(raw_data, taps, weight, *consts)
+    )(raw_data, fir_taps[None, :], spectral_weight[None, :], *consts)
     return result.transpose(1, 0, 2)
 
 

time: 112 us -> 110 us (0.982)
  Pallas kernels: 101 us -> 103 us
  local copies, waits for them, and re-layouts: 9.03 us -> 7.21 us
  other arithmetic: 1.3 us -> 0 us
    pallas_call x1, Pallas kernels: 101 us -> 103 us  [shards(): pl.pallas_call(corr_kernel, in_specs=[hbm] + [vmem] * 5, out_specs=hbm, o...]
    broadcast_in_dim x1 -> x0, other arithmetic: 1.3 us -> none  [shards(): weight = jnp.concatenate([spectral_weight, spectral_weight])[None, :]]
where the time goes in v3:
time: 110 us
  Pallas kernels  103 us (94%)
  local copies, waits for them, and re-layouts  7.21 us (7%)
    pallas_call x1, Pallas kernels, shards(): pl.pallas_call(corr_kernel, in_specs=[hbm] + [vmem] * 5, out_specs=hbm, o...  103 us
    unnamed x1, local copies, waits for them, and re-layouts  7.21 us

profile of v3, /device:TPU:1, one launch (start us, length us, event | category | flops | bytes accessed | tf_op | source)
XLA Modules:
  0.0 109.9 jit_solution(6972058172209476792)
XLA Ops:
  0.0 102.7 %corr.1 = f32[201,8,1280]{2,1,0:T(8,128)} custom-call(f32[1280,384]{1,0:T(8,128)} %raw_hbm.1, f32[1,33]{1,0:T(1,128)} %bitcast.4, f32[1,64]{1,0:T(1,128)} %bitcast.5, bf16[256,256]{1,0:T(8,128)(2,1)} %constant.6.clone.fwd, bf16[256,256]{1,0:T(8,128)(2,1)} %constant.7.clone.inv, bf16[384,256]{1,0:T(8,128)(2,1)} %constant.8.clone.band), custom_call_target="tpu_custom_call" | custom-call | tf_op jit(solution)/shard_map/corr/pallas_call | solution.py:503
  102.7 7.2 %copy.8 = f32[8,201,1280]{2,0,1:T(8,128)} copy(f32[8,201,1280]{2,0,1:T(8,128)} %bitcast.3) | data formatting | bytes 16465920

commit v4 on v3

--- a/solution.py
+++ b/solution.py
@@ -96,7 +96,7 @@
 
 
 AHEAD = 4
-HALOS_AHEAD = 7
+HALOS_AHEAD = 6
 LANES = 128
 COLS = 256
 ROWS = 128
@@ -376,14 +376,6 @@
     def near(c):
         @pl.when(c < steps)
         def _():
-            @pl.when(c + HALOS_AHEAD < steps)
-            def _():
-                on_sides(halo_pair(c + HALOS_AHEAD), "start")
-
-            @pl.when(c + AHEAD < steps)
-            def _():
-                whiten_step(c + AHEAD)
-
             arrived(c, 0, blk_p)
             start(c, "p")
 
@@ -394,6 +386,14 @@
             start(c, "u")
             arrived(c, 2, blk_d)
             start(c, "d")
+
+            @pl.when(c + HALOS_AHEAD < steps)
+            def _():
+                on_sides(halo_pair(c + HALOS_AHEAD), "start")
+
+            @pl.when(c + AHEAD < steps)
+            def _():
+                whiten_step(c + AHEAD)
 
         @pl.when((c >= 1) & (c <= steps))
         def _():

time: 110 us -> 105 us (0.955)
  Pallas kernels: 103 us -> 97.9 us
    pallas_call x1, Pallas kernels: 103 us -> 97.9 us  [shards(): pl.pallas_call(corr_kernel, in_specs=[hbm] + [vmem] * 5, out_specs=hbm, o...]
where the time goes in v4:
time: 105 us
  Pallas kernels  97.9 us (93%)
  local copies, waits for them, and re-layouts  7.21 us (7%)
    pallas_call x1, Pallas kernels, shards(): pl.pallas_call(corr_kernel, in_specs=[hbm] + [vmem] * 5, out_specs=hbm, o...  97.9 us
    unnamed x1, local copies, waits for them, and re-layouts  7.21 us

profile of v4, /device:TPU:1, one launch (start us, length us, event | category | flops | bytes accessed | tf_op | source)
XLA Modules:
  0.0 105.2 jit_solution(17082600788183248138)
XLA Ops:
  0.0 97.9 %corr.1 = f32[201,8,1280]{2,1,0:T(8,128)} custom-call(f32[1280,384]{1,0:T(8,128)} %raw_hbm.1, f32[1,33]{1,0:T(1,128)} %bitcast.4, f32[1,64]{1,0:T(1,128)} %bitcast.5, bf16[256,256]{1,0:T(8,128)(2,1)} %constant.6.clone.fwd, bf16[256,256]{1,0:T(8,128)(2,1)} %constant.7.clone.inv, bf16[384,256]{1,0:T(8,128)(2,1)} %constant.8.clone.band), custom_call_target="tpu_custom_call" | custom-call | tf_op jit(solution)/shard_map/corr/pallas_call | solution.py:503
  98.0 7.2 %copy.8 = f32[8,201,1280]{2,0,1:T(8,128)} copy(f32[8,201,1280]{2,0,1:T(8,128)} %bitcast.3) | data formatting | bytes 16465920
